TPU v7x, 32 devices: a whole 2x2x4 slice. The times are simulated.
32 devices in a mesh: grp: 2 (over y), row: 8 (over z, x), key: 2 (over core).
Axes of the slice: x: 2, y: 2, z: 4, core: 2. Of those that a mesh axis runs over, the one named last changes fastest.
Arguments:
- query: bfloat16 [32, 768, 128], P(('grp', 'row'), 'key'), parts along dimension 0, may hold values from -8 to 8
- keys: bfloat16 [32, 768, 128], P(('grp', 'row'), 'key'), parts along dimension 0, may hold values from -8 to 8
- values: bfloat16 [32, 768, 128], P(('grp', 'row'), 'key'), parts along dimension 0, may hold values from -6 to 6
- gate_logits: bfloat16 [32, 768, 128], P(('grp', 'row'), 'key'), parts along dimension 0, may hold values from -8 to 8
- pair_bias: bfloat16 [4, 1536, 768], P(None, ('grp', 'row'), 'key'), parts along dimension 1, may hold values from -6 to 6
- key_mask: int32 [1536], P(('grp', 'key')), parts along dimension 0, may hold values 0 or 1
- grad_out: bfloat16 [32, 768, 128], P(('grp', 'row'), 'key'), parts along dimension 0, may hold values from -6 to 6
Outputs:
- grad_query: bfloat16 [32, 768, 128], P(('grp', 'row'), 'key'), parts along dimension 0
- grad_keys: bfloat16 [32, 768, 128], P(('grp', 'row'), 'key'), parts along dimension 0
- grad_values: bfloat16 [32, 768, 128], P(('grp', 'row'), 'key'), parts along dimension 0
- grad_gate: bfloat16 [32, 768, 128], P(('grp', 'row'), 'key'), parts along dimension 0
- grad_bias: float32 [4, 1536, 768], P(None, ('grp', 'row'), 'key'), parts along dimension 1
There are 2 independent parts, one for each index of `grp`. A program takes and returns all parts, laid end to end along the dimension named above; each array names one. Nothing has to cross between parts.
All inputs are finite; a program needn't handle non-finite values. No bound on the sum of `key_mask` on one device may be relied on, other than what follows from the above.
Results may differ from a plain program's by a relative error of at most 0.024.
Values may be sent and summed in bfloat16 or wider, within the bound.
A program may use at most 64 MiB of HBM per device.

v0:
```python
import math

import jax
import jax.numpy as jnp
from jax import lax
from jax.sharding import PartitionSpec as P


def combined_all(value, axis, join):
    pieces = jax.tree.map(lambda part: lax.all_gather(part, axis), value)
    head = jax.tree.map(lambda part: part[0], pieces)
    tail = jax.tree.map(lambda part: part[1:], pieces)
    subtotal, _ = lax.scan(lambda subtotal, slab: (join(subtotal, slab), None), head, tail)
    return subtotal


def combine_stats(first, second):
    joint_max = jnp.maximum(first[0], second[0])
    joint_total = first[1] * jnp.exp(first[0] - joint_max) + second[1] * jnp.exp(
        second[0] - joint_max
    )
    return (joint_max, joint_total)


def shards(query, keys, values, gate_logits, pair_bias, key_mask, grad_out):
    row_count, key_count, channels = query.shape
    head_count = pair_bias.shape[0]
    head_size = channels // head_count
    scaling = 1.0 / math.sqrt(head_size)
    query_all, gate_all, cot_all = (
        lax.all_gather(query, "key", axis=1, tiled=True),
        lax.all_gather(gate_logits, "key", axis=1, tiled=True),
        lax.all_gather(grad_out, "key", axis=1, tiled=True),
    )
    query_count = query_all.shape[1]
    bias_all = lax.all_gather(pair_bias, "row", axis=1, tiled=True)
    mask_add = 1000000000.0 * (key_mask.astype(jnp.float32) - 1.0)
    bias_full = bias_all.astype(jnp.float32) + mask_add[None, None, :]

    def one_row(grad_acc, inputs):
        query_row, key_row, value_row, gate_row, cot_row, gate_own, cot_own = inputs
        query_heads = query_row.reshape(query_count, head_count, head_size)
        key_heads = key_row.reshape(key_count, head_count, head_size)
        value_heads = value_row.reshape(key_count, head_count, head_size)
        logits = (
            jnp.einsum("jhd,khd->hjk", query_heads, key_heads, preferred_element_type=jnp.float32)
            * scaling
            + bias_full
        )
        local_max = jnp.max(logits, axis=-1)
        local_total = jnp.sum(jnp.exp(logits - local_max[:, :, None]), axis=-1)
        row_max, row_total = combined_all((local_max, local_total), "key", combine_stats)
        softmax_out = jnp.exp(logits - row_max[:, :, None]) / row_total[:, :, None]
        softmax_low = softmax_out.astype(jnp.bfloat16)
        partial_out = jnp.einsum(
            "hjk,khd->jhd", softmax_low, value_heads, preferred_element_type=jnp.float32
        ).reshape(query_count, channels)
        gate_sig = jax.nn.sigmoid(gate_row.astype(jnp.float32))
        d_attended = (cot_row.astype(jnp.float32) * gate_sig).astype(jnp.bfloat16)
        upstream = d_attended.reshape(query_count, head_count, head_size)
        d_probs = jnp.einsum(
            "jhd,khd->hjk", upstream, value_heads, preferred_element_type=jnp.float32
        )
        own_out = lax.psum_scatter(partial_out, "key", scatter_dimension=0, tiled=True)
        inner = lax.psum(jnp.sum(softmax_low * d_probs, axis=-1), "key")
        own_sig = jax.nn.sigmoid(gate_own.astype(jnp.float32))
        gate_delta = (cot_own.astype(jnp.float32) * own_out * own_sig * (1.0 - own_sig)).astype(
            jnp.bfloat16
        )
        d_logits = softmax_out * (d_probs - inner[:, :, None])
        d_low = d_logits.astype(jnp.bfloat16)
        query_term = jnp.einsum(
            "hjk,khd->jhd", d_low, key_heads, preferred_element_type=jnp.float32
        ).reshape(query_count, channels)
        query_delta = (
            lax.psum_scatter(query_term, "key", scatter_dimension=0, tiled=True) * scaling
        ).astype(jnp.bfloat16)
        key_delta = (
            (
                jnp.einsum("hjk,jhd->khd", d_low, query_heads, preferred_element_type=jnp.float32)
                * scaling
            )
            .reshape(key_count, channels)
            .astype(jnp.bfloat16)
        )
        value_delta = (
            jnp.einsum("hjk,jhd->khd", softmax_low, upstream, preferred_element_type=jnp.float32)
            .reshape(key_count, channels)
            .astype(jnp.bfloat16)
        )
        return (grad_acc + d_logits, (query_delta, key_delta, value_delta, gate_delta))

    inputs_all = (query_all, keys, values, gate_all, cot_all, gate_logits, grad_out)
    empty_grad = jnp.zeros((head_count, query_count, key_count), jnp.float32)
    grad_acc, results = lax.scan(one_row, empty_grad, inputs_all)
    grad_bias = lax.psum_scatter(grad_acc, "row", scatter_dimension=1, tiled=True)
    return (results[0], results[1], results[2], results[3], grad_bias)


def solution(mesh):
    in_specs = (
        P(("grp", "row"), "key", None),
        P(("grp", "row"), "key", None),
        P(("grp", "row"), "key", None),
        P(("grp", "row"), "key", None),
        P(None, ("grp", "row"), "key"),
        P(("grp", "key")),
        P(("grp", "row"), "key", None),
    )
    out_specs = (
        P(("grp", "row"), "key", None),
        P(("grp", "row"), "key", None),
        P(("grp", "row"), "key", None),
        P(("grp", "row"), "key", None),
        P(None, ("grp", "row"), "key"),
    )
    return jax.shard_map(shards, mesh=mesh, in_specs=in_specs, out_specs=out_specs, check_vma=False)
```

profile of v0, /device:TPU:29, one launch (start us, length us, event | category | flops | bytes accessed | tf_op | source)
XLA Modules:
  0.0 262.3 jit_solution(18270461379729665808)
XLA Ops:
  7.2 1.8 copy.34
  9.1 1.1 copy.36
  10.2 1.7 copy.35
  11.9 1.1 copy.33
  13.0 2.4 all_gather.24
  15.4 3.9 %all_gather.26 = bf16[2,768,128]{1,2,0:T(8,128)(2,1)} all-gather(bf16[2,384,128]{1,2,0:T(8,128)(2,1)} %copy.35), channel_id=1, replica_groups=mesh['grp'=2,'row'=8,'key'=2] {'key'}, dimensions={1}, use_global_device_ids=true | all-gather | bytes 589824 | tf_op jit(solution)/shard_map/all_gather | solution.py:33
  19.3 2.2 all_gather.27
  21.5 0.7 add_multiply_fusion
  22.2 39.1 %all-gather.12.cloned.1.call-done = bf16[4,768,384]{2,0,1:T(4,128)(2,1)} async-done(((bf16[4,96,384]{2,0,1:T(4,128)(2,1)}), bf16[4,768,384]{2,0,1:T(4,128)(2,1)}) %all-gather.12.cloned.1.call-update) | async-done | bytes 2359312 | tf_op jit(solution)/shard_map/all_gather | solution.py:36
  61.4 4.7 %convert_add_fusion = f32[4,768,384]{2,0,1:T(4,128)} fusion(bf16[4,768,384]{2,0,1:T(4,128)(2,1)} %all-gather.12.cloned.1.call-done, f32[384]{0:T(512)S(1)} %add_multiply_fusion), kind=kLoop, calls=%fused_computation.37 | loop fusion | flops 2359296 | bytes 7079424 | tf_op jit(solution)/shard_map/add | solution.py:38
  66.1 6.7 %copy.38 = f32[4,768,384]{1,2,0:T(8,128)} copy(f32[4,768,384]{2,0,1:T(4,128)} %convert_add_fusion) | data formatting | bytes 9437184
  72.8 81.0 %while.16 = (s32[]{:T(128)}, f32[4,768,384]{1,2,0:T(8,128)}, bf16[2,384,128]{2,1,0:T(8,128)(2,1)}, bf16[2,384,128]{2,1,0:T(8,128)(2,1)}, bf16[2,384,128]{2,1,0:T...) while((s32[]{:T(128)}, f32[4,768,384]{1,2,0:T(8,128)}, ...), condition=%wide.region_7.8_spmd.clone, body=%wide.region_0.7_spmd.clone.sunk | while | flops 482734080 | bytes 88068424 | solution.py:95
  72.8 1.0 constant_dynamic-slice_fusion.6
  74.0 3.2 %fusion.59 = (f32[4,768]{1,0:T(4,128)S(1)}, f32[4,768,384]{1,2,0:T(8,128)S(1)}) fusion(f32[4,768,384]{1,2,0:T(8,128)} %get-tuple-element.367, bf16[768,4,32]{0,2,1:T(8,128)(2,1)S(1)} %bitcast.124, bf16[384,4,32]{0,2,1:T(8,128)(2,1)S(1)} %bitcast.127), kind=kOutput, calls=%fused_computation.39.clone.1 | convolution fusion | flops 79033344 | bytes 9744384 | tf_op jit(solution)/shard_map/while/body/eval_jaxpr/jhd,khd->hjk/dot_general | solution.py:46
  77.9 2.8 %all-gather.8 = f32[2,4,768]{2,1,0:T(4,128)S(1)} all-gather(f32[1,4,768]{2,1,0:T(4,128)S(1)} %bitcast.137), channel_id=3, replica_groups=mesh['grp'=2,'row'=8,'key'=2] {'key'}, dimensions={0}, use_global_device_ids=true | all-gather | bytes 36864 | tf_op jit(solution)/shard_map/while/body/eval_jaxpr/all_gather | solution.py:10
  80.7 1.8 all-gather.9
  82.5 1.7 fusion.65
  84.3 1.1 multiply_convert_fusion.3
  85.4 5.5 %multiply_reduce_fusion.2 = (f32[4,768]{1,0:T(4,128)S(1)}, f32[4,768,384]{1,2,0:T(8,128)}) fusion(f32[4,768]{1,0:T(4,128)S(1)} %get-tuple-element.320, f32[4,768,384]{1,2,0:T(8,128)} %copy-done, f32[4,768]{1,0:T(4,128)S(1)} %get-tuple-element.321, bf16[768,4,32]{0,2,1:T(8,128)(2,1)S(1)} %bitcast.131, bf16[384,4,32]{0,2,1:T(8,128)(2,1)S(1)} %bitcast.135), kind=kOutput, calls=%fused_computation.2.clone.1 | convolution fusion | flops 82572288 | bytes 9768960 | tf_op jit(solution)/shard_map/while/body/eval_jaxpr/jhd,khd->hjk/dot_general | solution.py:61
  90.9 3.5 %psum.9 = f32[4,768]{1,0:T(4,128)S(1)} all-reduce(f32[4,768]{1,0:T(4,128)S(1)} %get-tuple-element.324), channel_id=1, replica_groups=mesh['grp'=2,'row'=8,'key'=2] {'key'}, use_global_device_ids=true, to_apply=%region_4.4 | all-reduce | flops 3072 | bytes 24576 | tf_op jit(solution)/shard_map/while/body/eval_jaxpr/psum | solution.py:65
  94.4 6.0 %fusion.61 = (bf16[4,768,384]{1,2,0:T(8,128)(2,1)S(1)}, f32[4,768,384]{1,2,0:T(8,128)}) fusion(f32[4,768,384]{1,2,0:T(8,128)} %get-tuple-element.323, f32[4,768]{1,0:T(4,128)S(1)} %psum.9, f32[4,768]{1,0:T(4,128)S(1)} %get-tuple-element.320, f32[4,768,384]{1,2,0:T(8,128)} %copy-done, f32[4,768]{1,0:T(4,128)S(1)} %get-tuple-element.321, ...), kind=kLoop, calls=%fused_computation.6.clone.1 | loop fusion | flops 8257536 | bytes 21270528 | tf_op jit(solution)/shard_map/while/body/eval_jaxpr/convert_element_type | solution.py:71
  100.4 1.3 fusion.62
  101.7 3.2 %convolution_convert_fusion.2 = bf16[4,32,384]{2,1,0:T(8,128)(2,1)S(1)} fusion(bf16[768,4,32]{0,2,1:T(8,128)(2,1)S(1)} %bitcast.132, f32[4,768,384]{1,2,0:T(8,128)} %copy-done, f32[4,768]{1,0:T(4,128)S(1)} %get-tuple-element.320, f32[4,768]{1,0:T(4,128)} %copy-done.1), kind=kOutput, calls=%fused_computation.9.clone.1 | convolution fusion | flops 79085568 | bytes 5038080 | tf_op jit(solution)/shard_map/while/body/eval_jaxpr/hjk,jhd->khd/dot_general | solution.py:87
  105.1 0.8 fusion.64
  106.0 0.7 constant_dynamic-update-slice_fusion.10
  107.3 1.1 fusion.66
  108.5 1.4 reduce-scatter.6.cloned.1.call-done
  109.9 0.9 fusion.63
  111.0 0.7 constant_dynamic-update-slice_fusion.11
  112.3 1.0 constant_dynamic-slice_fusion.6
  113.6 3.2 %fusion.59 = (f32[4,768]{1,0:T(4,128)S(1)}, f32[4,768,384]{1,2,0:T(8,128)S(1)}) fusion(f32[4,768,384]{1,2,0:T(8,128)} %get-tuple-element.367, bf16[768,4,32]{0,2,1:T(8,128)(2,1)S(1)} %bitcast.124, bf16[384,4,32]{0,2,1:T(8,128)(2,1)S(1)} %bitcast.127), kind=kOutput, calls=%fused_computation.39.clone.1 | convolution fusion | flops 79033344 | bytes 9744384 | tf_op jit(solution)/shard_map/while/body/eval_jaxpr/jhd,khd->hjk/dot_general | solution.py:46
  117.4 1.8 all-gather.8
  119.2 1.8 all-gather.9
  121.1 1.7 fusion.65
  122.8 1.1 multiply_convert_fusion.3
  124.0 5.5 %multiply_reduce_fusion.2 = (f32[4,768]{1,0:T(4,128)S(1)}, f32[4,768,384]{1,2,0:T(8,128)}) fusion(f32[4,768]{1,0:T(4,128)S(1)} %get-tuple-element.320, f32[4,768,384]{1,2,0:T(8,128)} %copy-done, f32[4,768]{1,0:T(4,128)S(1)} %get-tuple-element.321, bf16[768,4,32]{0,2,1:T(8,128)(2,1)S(1)} %bitcast.131, bf16[384,4,32]{0,2,1:T(8,128)(2,1)S(1)} %bitcast.135), kind=kOutput, calls=%fused_computation.2.clone.1 | convolution fusion | flops 82572288 | bytes 9768960 | tf_op jit(solution)/shard_map/while/body/eval_jaxpr/jhd,khd->hjk/dot_general | solution.py:61
  129.5 3.3 %psum.9 = f32[4,768]{1,0:T(4,128)S(1)} all-reduce(f32[4,768]{1,0:T(4,128)S(1)} %get-tuple-element.324), channel_id=1, replica_groups=mesh['grp'=2,'row'=8,'key'=2] {'key'}, use_global_device_ids=true, to_apply=%region_4.4 | all-reduce | flops 3072 | bytes 24576 | tf_op jit(solution)/shard_map/while/body/eval_jaxpr/psum | solution.py:65
  132.8 8.1 %fusion.61 = (bf16[4,768,384]{1,2,0:T(8,128)(2,1)S(1)}, f32[4,768,384]{1,2,0:T(8,128)}) fusion(f32[4,768,384]{1,2,0:T(8,128)} %get-tuple-element.323, f32[4,768]{1,0:T(4,128)S(1)} %psum.9, f32[4,768]{1,0:T(4,128)S(1)} %get-tuple-element.320, f32[4,768,384]{1,2,0:T(8,128)} %copy-done, f32[4,768]{1,0:T(4,128)S(1)} %get-tuple-element.321, ...), kind=kLoop, calls=%fused_computation.6.clone.1 | loop fusion | flops 8257536 | bytes 21270528 | tf_op jit(solution)/shard_map/while/body/eval_jaxpr/convert_element_type | solution.py:71
  140.9 1.3 fusion.62
  142.2 3.2 %convolution_convert_fusion.2 = bf16[4,32,384]{2,1,0:T(8,128)(2,1)S(1)} fusion(bf16[768,4,32]{0,2,1:T(8,128)(2,1)S(1)} %bitcast.132, f32[4,768,384]{1,2,0:T(8,128)} %copy-done, f32[4,768]{1,0:T(4,128)S(1)} %get-tuple-element.320, f32[4,768]{1,0:T(4,128)} %copy-done.1), kind=kOutput, calls=%fused_computation.9.clone.1 | convolution fusion | flops 79085568 | bytes 5038080 | tf_op jit(solution)/shard_map/while/body/eval_jaxpr/hjk,jhd->khd/dot_general | solution.py:87
  145.5 0.8 fusion.64
  146.5 0.7 constant_dynamic-update-slice_fusion.10
  147.8 1.1 fusion.66
  149.0 2.5 reduce-scatter.6.cloned.1.call-done
  151.4 0.9 fusion.63
  152.5 0.7 constant_dynamic-update-slice_fusion.11
  153.8 6.1 %copy.42 = f32[4,768,384]{2,1,0:T(8,128)} copy(f32[4,768,384]{1,2,0:T(8,128)} %get-tuple-element.100) | data formatting | bytes 9437184 | tf_op jit(solution)/shard_map/while | solution.py:95
  159.9 95.6 %reduce-scatter.4.cloned.1.call-done = f32[4,96,384]{2,1,0:T(8,128)} async-done(((f32[4,768,384]{2,1,0:T(8,128)}), f32[4,96,384]{2,1,0:T(8,128)}) %reduce-scatter.4.cloned.1.call-update) | async-done | bytes 589840 | tf_op jit(solution)/shard_map/reduce_scatter | solution.py:96
  (49 shorter events, 5.7 us)
Async XLA Ops:
  7.2 54.2 %all-gather.12.cloned.1.call-start = ((), (), s32[]{:S(2)}) async-start(), calls=%async_computation.3 | async-start | bytes 2654208 | tf_op jit(solution)/shard_map/all_gather | solution.py:36
  72.8 34.5 %reduce-scatter.8.cloned.1.call-start = ((), (), s32[]{:S(2)}) async-start(), calls=%async_computation.6 | async-start | bytes 589824 | tf_op jit(solution)/shard_map/while/body/eval_jaxpr/reduce_scatter | solution.py:64
  77.2 7.0 %copy-start = (f32[4,768,384]{1,2,0:T(8,128)}, f32[4,768,384]{1,2,0:T(8,128)S(1)}, u32[]{:S(2)}) copy-start(f32[4,768,384]{1,2,0:T(8,128)S(1)} %get-tuple-element.318) | copy-start | bytes 14155780 | tf_op jit(solution)/shard_map/while
  82.5 11.9 %copy-start.1 = (f32[4,768]{1,0:T(4,128)}, f32[4,768]{1,0:T(4,128)S(1)}, u32[]{:S(2)}) copy-start(f32[4,768]{1,0:T(4,128)S(1)} %get-tuple-element.321) | copy-start | bytes 36868 | tf_op jit(solution)/shard_map/while
  84.2 25.7 %reduce-scatter.6.cloned.1.call-start = ((), (), s32[]{:S(2)}) async-start(), calls=%async_computation.5 | async-start | bytes 589824 | tf_op jit(solution)/shard_map/while/body/eval_jaxpr/reduce_scatter | solution.py:76
  112.3 35.4 %reduce-scatter.8.cloned.1.call-start = ((), (), s32[]{:S(2)}) async-start(), calls=%async_computation.6 | async-start | bytes 589824 | tf_op jit(solution)/shard_map/while/body/eval_jaxpr/reduce_scatter | solution.py:64
  116.7 6.0 %copy-start = (f32[4,768,384]{1,2,0:T(8,128)}, f32[4,768,384]{1,2,0:T(8,128)S(1)}, u32[]{:S(2)}) copy-start(f32[4,768,384]{1,2,0:T(8,128)S(1)} %get-tuple-element.318) | copy-start | bytes 14155780 | tf_op jit(solution)/shard_map/while
  121.1 11.7 %copy-start.1 = (f32[4,768]{1,0:T(4,128)}, f32[4,768]{1,0:T(4,128)S(1)}, u32[]{:S(2)}) copy-start(f32[4,768]{1,0:T(4,128)S(1)} %get-tuple-element.321) | copy-start | bytes 36868 | tf_op jit(solution)/shard_map/while
  122.8 28.7 %reduce-scatter.6.cloned.1.call-start = ((), (), s32[]{:S(2)}) async-start(), calls=%async_computation.5 | async-start | bytes 589824 | tf_op jit(solution)/shard_map/while/body/eval_jaxpr/reduce_scatter | solution.py:76
  153.8 101.6 %reduce-scatter.4.cloned.1.call-start = ((), (), s32[]{:S(2)}) async-start(), calls=%async_computation.4 | async-start | bytes 5308416 | tf_op jit(solution)/shard_map/reduce_scatter | solution.py:96
Sparse Core Ops, SparseCore 0:
  10.7 50.6 all-gather.11
  84.4 8.2 reduce-scatter.7
  101.8 8.0 reduce-scatter.5
  122.9 8.9 reduce-scatter.7
  142.3 9.0 reduce-scatter.5
  160.0 95.3 reduce-scatter.3
where the time goes:
time: 266 us; the launch traced here: 262 us
  waiting for transfers between devices  139 us (52%)
  matrix products  31.3 us (12%)
  local copies, waits for them, and re-layouts  27.2 us (10%)
  other arithmetic  27.2 us (10%)
  blocking collectives  23.5 us (9%)
  between operations  14.1 us (5%)
    reduce_scatter x1, waiting for transfers between devices, shards(): lax.psum_scatter(grad_acc, 'row', scatter_dimension=1, tiled=True)  95.6 us
    all_gather x1, waiting for transfers between devices, shards(): bias_all = lax.all_gather(pair_bias, 'row', axis=1, tiled=True)  39.1 us
    convert_element_type x2, other arithmetic, one_row(): d_low = d_logits.astype(jnp.bfloat16)  14.1 us
    unnamed x5, local copies, waits for them, and re-layouts  12.4 us
    dot_general x2, matrix products, one_row(): jnp.einsum('jhd,khd->hjk', upstream, value_heads, preferred_element_type=...  11 us
    all_gather x4, blocking collectives, combined_all(): pieces = jax.tree.map(lambda part: lax.all_gather(part, axis), value)  8.25 us
    psum x2, blocking collectives, one_row(): inner = lax.psum(jnp.sum(softmax_low * d_probs, axis=-1), 'key')  6.73 us
    dot_general x2, matrix products, one_row(): jnp.einsum('hjk,jhd->khd', softmax_low, upstream, preferred_element_type=...  6.42 us
  transfers between devices with their start and end apart: 6, of which 4 were waited for; matrix products, arithmetic and copies ran while one was open for 18% of the time, Pallas kernels for 0%

commit v1 on v0

--- a/solution.py
+++ b/solution.py
@@ -1,8 +1,11 @@
+import functools
 import math
 
 import jax
 import jax.numpy as jnp
 from jax import lax
+from jax.experimental import pallas as pl
+from jax.experimental.pallas import tpu as pltpu
 from jax.sharding import PartitionSpec as P
 
 
@@ -97,6 +100,339 @@
     return (results[0], results[1], results[2], results[3], grad_bias)
 
 
+def nt(a, b):
+    return lax.dot_general(a, b, (((1,), (1,)), ((), ())), preferred_element_type=jnp.float32)
+
+
+def nn(a, b):
+    return lax.dot_general(a, b, (((1,), (0,)), ((), ())), preferred_element_type=jnp.float32)
+
+
+def tn(a, b):
+    return lax.dot_general(a, b, (((0,), (0,)), ((), ())), preferred_element_type=jnp.float32)
+
+
+def fused_kernel(
+    groups, pair, cores,
+    q_ref, k_ref, v_ref, g_ref, o_ref, bias_ref, mask_ref,
+    dq_ref, dk_ref, dv_ref, dg_ref, db_ref,
+    xt, tt, mb, bb, q_tok, da_tok, gg_tok, dq_tok, dg_tok, dk_acc, dv_acc,
+    sb, rb, gs, gr, ot, orecv,
+    in_send, in_recv, bq_send, bq_recv, m_send, m_recv,
+    bl_send, br_send, b_recv, p_send, p_recv, g_send, g_recv, o_send, o_recv,
+):
+    row, core = lax.axis_index("row"), lax.axis_index("key")
+    zi, xi = row // pair, lax.rem(row, pair)
+    heads = pair * cores
+    me = xi * cores + core
+    own_rows, tokens, channels = q_ref.shape
+    width = channels // heads
+    rows = pair * own_rows
+    keys = cores * tokens
+    block = bias_ref.shape[1]
+    scaling = 1.0 / math.sqrt(width)
+
+    def at_quad(other):
+        return {"row": zi * pair + other // cores, "key": lax.rem(other, cores)}
+
+    def at_z(other):
+        return {"row": other * pair + xi, "key": core}
+
+    def remote(src, dst, send, recv, where):
+        return pltpu.make_async_remote_copy(
+            src_ref=src, dst_ref=dst, send_sem=send, recv_sem=recv,
+            device_id=where, device_id_type=pl.DeviceIdType.MESH,
+        )
+
+    barrier = pltpu.get_barrier_semaphore()
+    for step in range(1, heads):
+        pl.semaphore_signal(
+            barrier, inc=1, device_id=at_quad(lax.rem(me + step, heads)),
+            device_id_type=pl.DeviceIdType.MESH,
+        )
+    for step in range(1, groups):
+        pl.semaphore_signal(
+            barrier, inc=1, device_id=at_z(lax.rem(zi + step, groups)),
+            device_id_type=pl.DeviceIdType.MESH,
+        )
+    pl.semaphore_wait(barrier, heads - 1 + groups - 1)
+
+    def bias_quad(step):
+        to, src = lax.rem(me + step, heads), lax.rem(me + heads - step, heads)
+        out = remote(
+            bias_ref.at[to], bb.at[row, core], bq_send.at[step], bq_recv.at[step], at_quad(to)
+        )
+        inn = remote(
+            bias_ref.at[to],
+            bb.at[zi * pair + src // cores, lax.rem(src, cores)],
+            bq_send.at[step], bq_recv.at[step], at_quad(to),
+        )
+        return out, inn
+
+    for step in range(1, heads):
+        bias_quad(step)[0].start()
+    for other in range(1, cores):
+        to = lax.rem(core + other, cores)
+        remote(
+            mask_ref, mb.at[core], m_send.at[other], m_recv.at[other], {"row": row, "key": to}
+        ).start()
+    bb[row, core] = bias_ref[me]
+    mb[core] = mask_ref[...]
+
+    def in_quad(array, step):
+        to, src = lax.rem(me + step, heads), lax.rem(me + heads - step, heads)
+        out = remote(
+            xt.at[array, to], tt.at[array, xi, core],
+            in_send.at[array, step], in_recv.at[array, step], at_quad(to),
+        )
+        inn = remote(
+            xt.at[array, to], tt.at[array, src // cores, lax.rem(src, cores)],
+            in_send.at[array, step], in_recv.at[array, step], at_quad(to),
+        )
+        return out, inn
+
+    for array, ref in enumerate((q_ref, k_ref, v_ref, g_ref, o_ref)):
+        for local in range(own_rows):
+            turned = jnp.transpose(ref[local].astype(jnp.float32)).astype(jnp.bfloat16)
+            for head in range(heads):
+                xt[array, head, local] = turned[head * width : (head + 1) * width, :]
+        for step in range(1, heads):
+            in_quad(array, step)[0].start()
+        tt[array, xi, core] = xt[array, me]
+
+    for step in range(1, heads):
+        bias_quad(step)[1].wait_recv()
+
+    def slab(index):
+        return bb.at[pl.ds(index * pair, pair)]
+
+    def to_left(index):
+        return remote(slab(index), slab(index), bl_send.at[index], b_recv.at[index], at_z(zi - 1))
+
+    def to_right(index):
+        return remote(slab(index), slab(index), br_send.at[index], b_recv.at[index], at_z(zi + 1))
+
+    @pl.when(zi > 0)
+    def _():
+        to_left(zi).start()
+
+    @pl.when(zi < groups - 1)
+    def _():
+        to_right(zi).start()
+
+    for other in range(1, cores):
+        src = lax.rem(core + cores - other, cores)
+        to = lax.rem(core + other, cores)
+        remote(
+            mask_ref, mb.at[src], m_send.at[other], m_recv.at[other], {"row": row, "key": to}
+        ).wait()
+    for array in range(5):
+        for step in range(1, heads):
+            in_quad(array, step)[1].wait_recv()
+
+    def joined(array, index):
+        at, local = index // own_rows, index % own_rows
+        return jnp.concatenate([tt[array, at, c, local] for c in range(cores)], axis=1)
+
+    for index in range(rows):
+        q_tok[index] = jnp.transpose(joined(0, index).astype(jnp.float32)).astype(jnp.bfloat16)
+        sig = jax.nn.sigmoid(joined(3, index).astype(jnp.float32))
+        upstream = joined(4, index).astype(jnp.float32) * sig
+        low = upstream.astype(jnp.bfloat16).astype(jnp.float32)
+        da_tok[index] = jnp.transpose(low).astype(jnp.bfloat16)
+        gg_tok[index] = jnp.transpose(upstream * (1.0 - sig))
+        dk_acc[index] = jnp.zeros((width, keys), jnp.float32)
+        dv_acc[index] = jnp.zeros((width, keys), jnp.float32)
+
+    def queries(rblk):
+        mask = jnp.concatenate([mb[c] for c in range(cores)], axis=1).astype(jnp.float32)
+        bias = jnp.concatenate([bb[rblk, c] for c in range(cores)], axis=1).astype(jnp.float32)
+        bias = bias + 1000000000.0 * (mask - 1.0)
+        here = pl.ds(pl.multiple_of(rblk * block, 32), block)
+        total = None
+        for index in range(rows):
+            kt, vt = joined(1, index), joined(2, index)
+            q, da = q_tok[index, here, :], da_tok[index, here, :]
+            logits = nn(q, kt) * scaling + bias
+            expo = jnp.exp(logits - jnp.max(logits, axis=-1, keepdims=True))
+            probs = expo * (1.0 / jnp.sum(expo, axis=-1, keepdims=True))
+            low = probs.astype(jnp.bfloat16)
+            attended = nt(low, vt)
+            inner = jnp.sum(da.astype(jnp.float32) * attended, axis=-1, keepdims=True)
+            d_logits = probs * (nn(da, vt) - inner)
+            d_low = d_logits.astype(jnp.bfloat16)
+            dq_tok[index, here, :] = nt(d_low, kt) * scaling
+            dg_tok[index, here, :] = attended * gg_tok[index, here, :]
+            dk_acc[index] += tn(q, d_low)
+            dv_acc[index] += tn(da, low)
+            total = d_logits if total is None else total + d_logits
+        for c in range(cores):
+            sb[rblk, c] = total[:, c * tokens : (c + 1) * tokens].astype(jnp.bfloat16)
+
+    def partial_out(index):
+        return remote(
+            sb.at[pl.ds(index * pair, pair)], rb.at[zi], p_send.at[index], p_recv.at[zi],
+            at_z(index),
+        )
+
+    orders = [sorted(range(groups), key=lambda b, a=a: abs(b - a)) for a in range(groups)]
+
+    def turn(step, carry):
+        left, right = zi - step, zi + step
+
+        @pl.when(jnp.logical_and(step > 0, left >= 0))
+        def _():
+            to_left(left).wait_recv()
+
+        @pl.when(jnp.logical_and(jnp.logical_and(step > 0, left >= 0), zi < groups - 1))
+        def _():
+            to_right(left).start()
+
+        @pl.when(jnp.logical_and(step > 0, right < groups))
+        def _():
+            to_right(right).wait_recv()
+
+        @pl.when(jnp.logical_and(jnp.logical_and(step > 0, right < groups), zi > 0))
+        def _():
+            to_left(right).start()
+
+        index = jnp.int32(0)
+        for a in range(groups):
+            for s in range(groups):
+                hit = jnp.logical_and(zi == a, step == s)
+                index = jnp.where(hit, orders[a][s], index)
+        for part in range(pair):
+            queries(index * pair + part)
+
+        @pl.when(index != zi)
+        def _():
+            partial_out(index).start()
+
+        return carry
+
+    lax.fori_loop(0, groups, turn, 0)
+
+    for index in range(rows):
+        at, local = index // own_rows, index % own_rows
+        whole = (
+            jnp.transpose(dq_tok[index]),
+            dk_acc[index] * scaling,
+            dv_acc[index],
+            jnp.transpose(dg_tok[index]),
+        )
+        for array, value in enumerate(whole):
+            value = value.astype(jnp.bfloat16)
+            for c in range(cores):
+                ot[at, c, array, local] = value[:, c * tokens : (c + 1) * tokens]
+
+    def out_quad(step):
+        to, src = lax.rem(me + step, heads), lax.rem(me + heads - step, heads)
+        away = ot.at[to // cores, lax.rem(to, cores)]
+        out = remote(away, orecv.at[me], o_send.at[step], o_recv.at[step], at_quad(to))
+        inn = remote(away, orecv.at[src], o_send.at[step], o_recv.at[step], at_quad(to))
+        return out, inn
+
+    for step in range(1, heads):
+        out_quad(step)[0].start()
+    orecv[me] = ot[xi, core]
+
+    for step in range(1, groups):
+        src = lax.rem(zi + step, groups)
+        remote(
+            sb.at[pl.ds(zi * pair, pair)], rb.at[src], p_send.at[src], p_recv.at[src], at_z(src)
+        ).wait_recv()
+    for part in range(pair):
+        for c in range(cores):
+            value = sb[zi * pair + part, c].astype(jnp.float32)
+            for step in range(1, groups):
+                value += rb[lax.rem(zi + step, groups), part, c].astype(jnp.float32)
+            gs[part, c] = value.astype(jnp.bfloat16)
+
+    def bias_out(step):
+        to, src = lax.rem(me + step, heads), lax.rem(me + heads - step, heads)
+        away = gs.at[to // cores, lax.rem(to, cores)]
+        out = remote(away, gr.at[me], g_send.at[step], g_recv.at[step], at_quad(to))
+        inn = remote(away, gr.at[src], g_send.at[step], g_recv.at[step], at_quad(to))
+        return out, inn
+
+    for step in range(1, heads):
+        bias_out(step)[0].start()
+    gr[me] = gs[xi, core]
+
+    for step in range(1, heads):
+        out_quad(step)[1].wait_recv()
+    for array, ref in enumerate((dq_ref, dk_ref, dv_ref, dg_ref)):
+        for local in range(own_rows):
+            tall = jnp.concatenate([orecv[head, array, local] for head in range(heads)], axis=0)
+            ref[local] = jnp.transpose(tall.astype(jnp.float32)).astype(jnp.bfloat16)
+    for step in range(1, heads):
+        bias_out(step)[1].wait_recv()
+    db_ref[...] = gr[...].astype(jnp.float32)
+
+    for step in range(1, heads):
+        bias_quad(step)[0].wait_send()
+        out_quad(step)[0].wait_send()
+        bias_out(step)[0].wait_send()
+        for array in range(5):
+            in_quad(array, step)[0].wait_send()
+    for step in range(1, groups):
+        index = lax.rem(zi + step, groups)
+        partial_out(index).wait_send()
+    for index in range(groups):
+
+        @pl.when(jnp.logical_and(zi > 0, index >= zi))
+        def _(index=index):
+            to_left(index).wait_send()
+
+        @pl.when(jnp.logical_and(zi < groups - 1, index <= zi))
+        def _(index=index):
+            to_right(index).wait_send()
+
+
+def fused(row_size, cores, query, keys, values, gate_logits, pair_bias, key_mask, grad_out):
+    heads, block, tokens = pair_bias.shape
+    own_rows, _, channels = query.shape
+    pair = heads // cores
+    groups = row_size // pair
+    rows, width, whole = pair * own_rows, channels // heads, cores * tokens
+    blocks = groups * pair
+    low, full, dma = jnp.bfloat16, jnp.float32, pltpu.SemaphoreType.DMA
+    grad = jax.ShapeDtypeStruct(query.shape, low)
+    vmem = pl.BlockSpec(memory_space=pltpu.VMEM)
+    return pl.pallas_call(
+        functools.partial(fused_kernel, groups, pair, cores),
+        out_shape=(grad, grad, grad, grad, jax.ShapeDtypeStruct(pair_bias.shape, full)),
+        in_specs=[vmem] * 7,
+        out_specs=[vmem] * 5,
+        scratch_shapes=[
+            pltpu.VMEM((5, heads, own_rows, width, tokens), low),
+            pltpu.VMEM((5, pair, cores, own_rows, width, tokens), low),
+            pltpu.VMEM((cores, 1, tokens), jnp.int32),
+            pltpu.VMEM((blocks, cores, block, tokens), low),
+            pltpu.VMEM((rows, whole, width), low),
+            pltpu.VMEM((rows, whole, width), low),
+            pltpu.VMEM((rows, whole, width), full),
+            pltpu.VMEM((rows, whole, width), full),
+            pltpu.VMEM((rows, whole, width), full),
+            pltpu.VMEM((rows, width, whole), full),
+            pltpu.VMEM((rows, width, whole), full),
+            pltpu.VMEM((blocks, cores, block, tokens), low),
+            pltpu.VMEM((groups, pair, cores, block, tokens), low),
+            pltpu.VMEM((pair, cores, block, tokens), low),
+            pltpu.VMEM((heads, block, tokens), low),
+            pltpu.VMEM((pair, cores, 4, own_rows, width, tokens), low),
+            pltpu.VMEM((heads, 4, own_rows, width, tokens), low),
+            dma((5, heads)), dma((5, heads)), dma((heads,)), dma((heads,)),
+            dma((cores,)), dma((cores,)),
+            dma((groups,)), dma((groups,)), dma((groups,)), dma((groups,)), dma((groups,)),
+            dma((heads,)), dma((heads,)), dma((heads,)), dma((heads,)),
+        ],
+        compiler_params=pltpu.CompilerParams(
+            collective_id=0, has_side_effects=True, vmem_limit_bytes=58 << 20
+        ),
+    )(query, keys, values, gate_logits, grad_out, pair_bias, key_mask.reshape(1, tokens))
+
+
 def solution(mesh):
     in_specs = (
         P(("grp", "row"), "key", None),
@@ -114,4 +450,14 @@
         P(("grp", "row"), "key", None),
         P(None, ("grp", "row"), "key"),
     )
-    return jax.shard_map(shards, mesh=mesh, in_specs=in_specs, out_specs=out_specs, check_vma=False)
+    row_size, cores = mesh.shape["row"], mesh.shape["key"]
+
+    def run(*arrays):
+        heads, block, tokens = arrays[4].shape
+        pair = max(heads // cores, 1)
+        aligned = block % 32 == 0 and tokens % 128 == 0
+        if aligned and heads == pair * cores and row_size % pair == 0:
+            return fused(row_size, cores, *arrays)
+        return shards(*arrays)
+
+    return jax.shard_map(run, mesh=mesh, in_specs=in_specs, out_specs=out_specs, check_vma=False)

time: 266 us -> 79.2 us (0.30); the launches traced: 262 us -> 79 us
  waiting for transfers between devices: 139 us -> 0 us
  Pallas kernels: 0 us -> 72.2 us
  matrix products: 31.3 us -> 0 us
  other arithmetic: 27.2 us -> 0 us
  blocking collectives: 23.5 us -> 0 us
  local copies, waits for them, and re-layouts: 27.2 us -> 6.09 us
  between operations: 14.1 us -> 0.66 us
    reduce_scatter x5 -> x0, waiting for transfers between devices: 99.5 us -> none  [the longest x1 95.6 us: shards(): lax.psum_scatter(grad_acc, 'row', scatter_dimension=1, tiled=True)]
    pallas_call x0 -> x1, Pallas kernels: none -> 72.2 us  [fused(): pl.pallas_call(functools.partial(fused_kernel, groups, pair, cores), out_...]
    all_gather x1 -> x0, waiting for transfers between devices: 39.1 us -> none  [shards(): bias_all = lax.all_gather(pair_bias, 'row', axis=1, tiled=True)]
    dot_general x12 -> x0, matrix products: 31.3 us -> none  [the longest x2 11 us: one_row(): jnp.einsum('jhd,khd->hjk', upstream, value_heads, preferred_element_type=...]
    all_gather x7 -> x0, blocking collectives: 16.8 us -> none  [the longest x4 8.25 us: combined_all(): pieces = jax.tree.map(lambda part: lax.all_gather(part, axis), value)]
    convert_element_type x4 -> x0, other arithmetic: 16.4 us -> none  [the longest x2 14.1 us: one_row(): d_low = d_logits.astype(jnp.bfloat16)]
    unnamed x5 -> x13, local copies, waits for them, and re-layouts: 12.4 us -> 4.84 us
    psum x2 -> x0, blocking collectives: 6.73 us -> none  [one_row(): inner = lax.psum(jnp.sum(softmax_low * d_probs, axis=-1), 'key')]
  transfers between devices with their start and end apart: 6 -> 0, of which waited for: 4 -> 0; matrix products, arithmetic and copies ran while one was open for 18% -> 0% of each run, Pallas kernels for 0% -> 0%
where the time goes in v1:
time: 79.2 us; the launch traced here: 79 us
  Pallas kernels  72.2 us (91%)
  local copies, waits for them, and re-layouts  6.09 us (8%)
    pallas_call x1, Pallas kernels, fused(): pl.pallas_call(functools.partial(fused_kernel, groups, pair, cores), out_...  72.2 us
    unnamed x13, local copies, waits for them, and re-layouts  4.84 us

profile of v1, /device:TPU:29, one launch (start us, length us, event | category | flops | bytes accessed | tf_op | source)
XLA Modules:
  0.0 79.0 jit_solution(8547465510210037566)
XLA Ops:
  0.6 1.2 %reshape.13.mask_ref = s32[1,384]{1,0:T(1,128)} reshape(s32[384]{0:T(512)} %param.12) | data formatting | bytes 3072 | tf_op jit(solution)/shard_map/reshape | solution.py:433
  1.9 72.2 %shard_map.110 = (bf16[2,384,128]{2,1,0:T(8,128)(2,1)}, bf16[2,384,128]{2,1,0:T(8,128)(2,1)}, bf16[2,384,128]{2,1,0:T(8,128)(2,1)}, bf16[2,384,128]{2,1,0:T(8,128)(2,1)}, f32[4,96,384]{2,1,0:T(8,128)}) custom-call(bf16[2,384,128]{2,1,0:T(8,128)(2,1)} %q_ref.1, bf16[2,384,128]{2,1,0:T(8,128)(2,1)} %k_ref.1, bf16[2,384,128]{2,1,0:T(8,128)(2,1)} %v_ref.1, ...), custom_call_target="tpu_custom_call" | custom-call | tf_op jit(solution)/shard_map/pallas_call | solution.py:402
  74.1 0.0 copy-start.3
  74.1 0.0 copy-start.2
  74.1 1.7 %copy.17 = bf16[2,384,128]{2,1,0:T(8,128)(2,1)} copy(bf16[2,384,128]{2,1,0:T(8,128)(2,1)} %get-tuple-element.10) | data formatting | bytes 393216
  75.8 0.0 copy-done.3
  75.8 0.0 copy-start
  75.8 0.7 copy.18
  76.5 0.0 copy-done.2
  76.5 0.0 copy-start.1
  76.5 0.7 copy.19
  77.2 0.3 copy-done.1
  77.5 0.7 copy.20
  78.2 0.0 copy-done
  78.2 0.8 %copy.21 = f32[4,96,384]{2,1,0:T(8,128)} copy(f32[4,96,384]{2,1,0:T(8,128)S(1)} %copy-done) | data formatting | bytes 1179648
Async XLA Ops:
  74.1 1.7 %copy-start.3 = (bf16[2,384,128]{2,1,0:T(8,128)(2,1)S(1)}, bf16[2,384,128]{2,1,0:T(8,128)(2,1)}, u32[]{:S(2)}) copy-start(bf16[2,384,128]{2,1,0:T(8,128)(2,1)} %get-tuple-element.11) | copy-start | bytes 589828
  74.1 2.4 %copy-start.2 = (bf16[2,384,128]{2,1,0:T(8,128)(2,1)S(1)}, bf16[2,384,128]{2,1,0:T(8,128)(2,1)}, u32[]{:S(2)}) copy-start(bf16[2,384,128]{2,1,0:T(8,128)(2,1)} %get-tuple-element.12) | copy-start | bytes 589828
  75.8 2.4 %copy-start = (f32[4,96,384]{2,1,0:T(8,128)S(1)}, f32[4,96,384]{2,1,0:T(8,128)}, u32[]{:S(2)}) copy-start(f32[4,96,384]{2,1,0:T(8,128)} %get-tuple-element.14) | copy-start | bytes 1769476
  76.5 1.0 %copy-start.1 = (bf16[2,384,128]{2,1,0:T(8,128)(2,1)S(1)}, bf16[2,384,128]{2,1,0:T(8,128)(2,1)}, u32[]{:S(2)}) copy-start(bf16[2,384,128]{2,1,0:T(8,128)(2,1)} %get-tuple-element.13) | copy-start | bytes 589828

commit v2 on v1

--- a/solution.py
+++ b/solution.py
@@ -115,11 +115,10 @@
 def fused_kernel(
     groups, pair, cores,
     q_ref, k_ref, v_ref, g_ref, o_ref, bias_ref, mask_ref,
-    dq_ref, dk_ref, dv_ref, dg_ref, db_ref,
-    xt, tt, mb, bb, q_tok, da_tok, gg_tok, dq_tok, dg_tok, dk_acc, dv_acc,
-    sb, rb, gs, gr, ot, orecv,
+    orecv, gr,
+    xt, tt, ms, mb, bb, q_tok, da_tok, dq_tok, at_tok, dk_acc, dv_acc, sb, rb, gs, ot,
     in_send, in_recv, bq_send, bq_recv, m_send, m_recv,
-    bl_send, br_send, b_recv, p_send, p_recv, g_send, g_recv, o_send, o_recv,
+    bl_send, br_send, b_recv, p_send, p_recv, g_send, g_recv, o_send, o_recv, local_sem,
 ):
     row, core = lax.axis_index("row"), lax.axis_index("key")
     zi, xi = row // pair, lax.rem(row, pair)
@@ -155,92 +154,133 @@
             barrier, inc=1, device_id=at_z(lax.rem(zi + step, groups)),
             device_id_type=pl.DeviceIdType.MESH,
         )
+
+    def turned(array):
+        for local in range(own_rows):
+            if array < 3:
+                value = (q_ref, k_ref, v_ref)[array][local]
+            else:
+                sig = jax.nn.sigmoid(g_ref[local].astype(jnp.float32))
+                value = (o_ref[local].astype(jnp.float32) * sig).astype(jnp.bfloat16)
+            value = jnp.transpose(value)
+            for head in range(heads):
+                xt[array, head, local] = value[head * width : (head + 1) * width, :]
+
+    own_bias = pltpu.make_async_copy(bias_ref.at[me], bb.at[row, core], local_sem.at[0])
+    own_bias.start()
+    ms[...] = mask_ref[...].reshape(1, tokens)
+    turned(0)
     pl.semaphore_wait(barrier, heads - 1 + groups - 1)
 
-    def bias_quad(step):
-        to, src = lax.rem(me + step, heads), lax.rem(me + heads - step, heads)
-        out = remote(
-            bias_ref.at[to], bb.at[row, core], bq_send.at[step], bq_recv.at[step], at_quad(to)
-        )
-        inn = remote(
-            bias_ref.at[to],
-            bb.at[zi * pair + src // cores, lax.rem(src, cores)],
-            bq_send.at[step], bq_recv.at[step], at_quad(to),
-        )
-        return out, inn
-
-    for step in range(1, heads):
-        bias_quad(step)[0].start()
-    for other in range(1, cores):
-        to = lax.rem(core + other, cores)
-        remote(
-            mask_ref, mb.at[core], m_send.at[other], m_recv.at[other], {"row": row, "key": to}
-        ).start()
-    bb[row, core] = bias_ref[me]
-    mb[core] = mask_ref[...]
-
-    def in_quad(array, step):
-        to, src = lax.rem(me + step, heads), lax.rem(me + heads - step, heads)
-        out = remote(
+    def bias_out_of(step):
+        to = lax.rem(me + step, heads)
+        return remote(
+            bias_ref.at[to], bb.at[row, core], bq_send.at[step], bq_recv.at[me], at_quad(to)
+        )
+
+    def bias_from(src):
+        return remote(
+            bias_ref.at[src], bb.at[zi * pair + src // cores, lax.rem(src, cores)],
+            bq_send.at[0], bq_recv.at[src], at_quad(src),
+        )
+
+    def mask_copy(other, src):
+        return remote(
+            ms, mb.at[src], m_send.at[other], m_recv.at[other],
+            {"row": row, "key": lax.rem(core + other, cores)},
+        )
+
+    def token_out(array, step):
+        to = lax.rem(me + step, heads)
+        return remote(
             xt.at[array, to], tt.at[array, xi, core],
             in_send.at[array, step], in_recv.at[array, step], at_quad(to),
         )
-        inn = remote(
-            xt.at[array, to], tt.at[array, src // cores, lax.rem(src, cores)],
-            in_send.at[array, step], in_recv.at[array, step], at_quad(to),
-        )
-        return out, inn
-
-    for array, ref in enumerate((q_ref, k_ref, v_ref, g_ref, o_ref)):
-        for local in range(own_rows):
-            turned = jnp.transpose(ref[local].astype(jnp.float32)).astype(jnp.bfloat16)
-            for head in range(heads):
-                xt[array, head, local] = turned[head * width : (head + 1) * width, :]
+
+    def token_in(array, step):
+        src = lax.rem(me + heads - step, heads)
+        return remote(
+            xt.at[array, src], tt.at[array, src // cores, lax.rem(src, cores)],
+            in_send.at[array, step], in_recv.at[array, step], at_quad(src),
+        )
+
+    def to_left(at):
+        return remote(bb.at[at], bb.at[at], bl_send.at[at], b_recv.at[at], at_z(zi - 1))
+
+    def to_right(at):
+        return remote(bb.at[at], bb.at[at], br_send.at[at], b_recv.at[at], at_z(zi + 1))
+
+    def launch(at):
+        @pl.when(zi > 0)
+        def _():
+            to_left(at).start()
+
+        @pl.when(zi < groups - 1)
+        def _():
+            to_right(at).start()
+
+    def relay(distance):
+        left, right = zi - distance, zi + distance
+        for step in range(pair):
+            part = lax.rem(xi + step, pair)
+
+            @pl.when(left >= 0)
+            def _(part=part):
+                to_left(left * pair + part).wait_recv()
+
+            @pl.when(jnp.logical_and(left >= 0, zi < groups - 1))
+            def _(part=part):
+                to_right(left * pair + part).start()
+
+            @pl.when(right < groups)
+            def _(part=part):
+                to_right(right * pair + part).wait_recv()
+
+            @pl.when(jnp.logical_and(right < groups, zi > 0))
+            def _(part=part):
+                to_left(right * pair + part).start()
+
+    for step in range(1, heads):
+        bias_out_of(step).start()
+    for other in range(1, cores):
+        mask_copy(other, core).start()
+    mb[core] = ms[...]
+    for step in range(1, heads):
+        token_out(0, step).start()
+    turned(1)
+    for step in range(1, heads):
+        token_out(1, step).start()
+    own_bias.wait()
+    for other in range(1, cores):
+        bias_from(xi * cores + lax.rem(core + other, cores)).wait_recv()
+    launch(row)
+    for array in range(2, 4):
+        turned(array)
         for step in range(1, heads):
-            in_quad(array, step)[0].start()
+            token_out(array, step).start()
+    for step in range(1, pair):
+        side = lax.rem(xi + step, pair)
+        for other in range(cores):
+            bias_from(side * cores + other).wait_recv()
+        launch(zi * pair + side)
+    for array in range(4):
         tt[array, xi, core] = xt[array, me]
-
-    for step in range(1, heads):
-        bias_quad(step)[1].wait_recv()
-
-    def slab(index):
-        return bb.at[pl.ds(index * pair, pair)]
-
-    def to_left(index):
-        return remote(slab(index), slab(index), bl_send.at[index], b_recv.at[index], at_z(zi - 1))
-
-    def to_right(index):
-        return remote(slab(index), slab(index), br_send.at[index], b_recv.at[index], at_z(zi + 1))
-
-    @pl.when(zi > 0)
-    def _():
-        to_left(zi).start()
-
-    @pl.when(zi < groups - 1)
-    def _():
-        to_right(zi).start()
-
     for other in range(1, cores):
-        src = lax.rem(core + cores - other, cores)
-        to = lax.rem(core + other, cores)
-        remote(
-            mask_ref, mb.at[src], m_send.at[other], m_recv.at[other], {"row": row, "key": to}
-        ).wait()
-    for array in range(5):
+        mask_copy(other, lax.rem(core + cores - other, cores)).wait()
+    early = min(2, groups - 1)
+    if early > 0:
+        relay(1)
+    for array in range(4):
         for step in range(1, heads):
-            in_quad(array, step)[1].wait_recv()
+            token_in(array, step).wait_recv()
 
     def joined(array, index):
         at, local = index // own_rows, index % own_rows
         return jnp.concatenate([tt[array, at, c, local] for c in range(cores)], axis=1)
 
     for index in range(rows):
-        q_tok[index] = jnp.transpose(joined(0, index).astype(jnp.float32)).astype(jnp.bfloat16)
-        sig = jax.nn.sigmoid(joined(3, index).astype(jnp.float32))
-        upstream = joined(4, index).astype(jnp.float32) * sig
-        low = upstream.astype(jnp.bfloat16).astype(jnp.float32)
-        da_tok[index] = jnp.transpose(low).astype(jnp.bfloat16)
-        gg_tok[index] = jnp.transpose(upstream * (1.0 - sig))
+        q_tok[index] = jnp.transpose(joined(0, index))
+        da_tok[index] = jnp.transpose(joined(3, index))
         dk_acc[index] = jnp.zeros((width, keys), jnp.float32)
         dv_acc[index] = jnp.zeros((width, keys), jnp.float32)
 
@@ -262,39 +302,30 @@
             d_logits = probs * (nn(da, vt) - inner)
             d_low = d_logits.astype(jnp.bfloat16)
             dq_tok[index, here, :] = nt(d_low, kt) * scaling
-            dg_tok[index, here, :] = attended * gg_tok[index, here, :]
+            at_tok[index, here, :] = attended
             dk_acc[index] += tn(q, d_low)
             dv_acc[index] += tn(da, low)
             total = d_logits if total is None else total + d_logits
         for c in range(cores):
             sb[rblk, c] = total[:, c * tokens : (c + 1) * tokens].astype(jnp.bfloat16)
 
-    def partial_out(index):
-        return remote(
-            sb.at[pl.ds(index * pair, pair)], rb.at[zi], p_send.at[index], p_recv.at[zi],
-            at_z(index),
-        )
-
-    orders = [sorted(range(groups), key=lambda b, a=a: abs(b - a)) for a in range(groups)]
+    def partial_out(index, part):
+        return remote(
+            sb.at[index * pair + part], rb.at[zi, part], p_send.at[index, part],
+            p_recv.at[zi, part], at_z(index),
+        )
+
+    orders = [
+        sorted(range(groups), key=lambda b, a=a: abs(b - a) if b != a else groups)
+        for a in range(groups)
+    ]
+    for distance in range(2, early + 1):
+        relay(distance)
 
     def turn(step, carry):
-        left, right = zi - step, zi + step
-
-        @pl.when(jnp.logical_and(step > 0, left >= 0))
+        @pl.when(jnp.logical_and(step >= early, step < groups - 1))
         def _():
-            to_left(left).wait_recv()
-
-        @pl.when(jnp.logical_and(jnp.logical_and(step > 0, left >= 0), zi < groups - 1))
-        def _():
-            to_right(left).start()
-
-        @pl.when(jnp.logical_and(step > 0, right < groups))
-        def _():
-            to_right(right).wait_recv()
-
-        @pl.when(jnp.logical_and(jnp.logical_and(step > 0, right < groups), zi > 0))
-        def _():
-            to_left(right).start()
+            relay(step + 1)
 
         index = jnp.int32(0)
         for a in range(groups):
@@ -304,9 +335,9 @@
         for part in range(pair):
             queries(index * pair + part)
 
-        @pl.when(index != zi)
-        def _():
-            partial_out(index).start()
+            @pl.when(index != zi)
+            def _(part=part):
+                partial_out(index, part).start()
 
         return carry
 
@@ -318,75 +349,101 @@
             jnp.transpose(dq_tok[index]),
             dk_acc[index] * scaling,
             dv_acc[index],
-            jnp.transpose(dg_tok[index]),
+            jnp.transpose(at_tok[index]),
         )
         for array, value in enumerate(whole):
             value = value.astype(jnp.bfloat16)
             for c in range(cores):
                 ot[at, c, array, local] = value[:, c * tokens : (c + 1) * tokens]
 
-    def out_quad(step):
-        to, src = lax.rem(me + step, heads), lax.rem(me + heads - step, heads)
-        away = ot.at[to // cores, lax.rem(to, cores)]
-        out = remote(away, orecv.at[me], o_send.at[step], o_recv.at[step], at_quad(to))
-        inn = remote(away, orecv.at[src], o_send.at[step], o_recv.at[step], at_quad(to))
-        return out, inn
-
-    for step in range(1, heads):
-        out_quad(step)[0].start()
-    orecv[me] = ot[xi, core]
-
-    for step in range(1, groups):
-        src = lax.rem(zi + step, groups)
-        remote(
-            sb.at[pl.ds(zi * pair, pair)], rb.at[src], p_send.at[src], p_recv.at[src], at_z(src)
-        ).wait_recv()
+    def grads_out(step):
+        to = lax.rem(me + step, heads)
+        return remote(
+            ot.at[to // cores, lax.rem(to, cores)], orecv.at[me],
+            o_send.at[step], o_recv.at[step], at_quad(to),
+        )
+
+    def grads_in(step):
+        src = lax.rem(me + heads - step, heads)
+        return remote(
+            ot.at[src // cores, lax.rem(src, cores)], orecv.at[src],
+            o_send.at[step], o_recv.at[step], at_quad(src),
+        )
+
+    def sum_out(step):
+        to = lax.rem(me + step, heads)
+        return remote(
+            gs.at[to // cores, lax.rem(to, cores)], gr.at[me],
+            g_send.at[step], g_recv.at[step], at_quad(to),
+        )
+
+    def sum_in(step):
+        src = lax.rem(me + heads - step, heads)
+        return remote(
+            gs.at[src // cores, lax.rem(src, cores)], gr.at[src],
+            g_send.at[step], g_recv.at[step], at_quad(src),
+        )
+
+    for step in range(1, heads):
+        grads_out(step).start()
+    own_grads = pltpu.make_async_copy(ot.at[xi, core], orecv.at[me], local_sem.at[1])
+    own_grads.start()
+
     for part in range(pair):
+        for step in range(1, groups):
+            src = lax.rem(zi + step, groups)
+            remote(
+                sb.at[zi * pair + part], rb.at[src, part], p_send.at[src, part],
+                p_recv.at[src, part], at_z(src),
+            ).wait_recv()
         for c in range(cores):
             value = sb[zi * pair + part, c].astype(jnp.float32)
             for step in range(1, groups):
                 value += rb[lax.rem(zi + step, groups), part, c].astype(jnp.float32)
             gs[part, c] = value.astype(jnp.bfloat16)
-
-    def bias_out(step):
-        to, src = lax.rem(me + step, heads), lax.rem(me + heads - step, heads)
-        away = gs.at[to // cores, lax.rem(to, cores)]
-        out = remote(away, gr.at[me], g_send.at[step], g_recv.at[step], at_quad(to))
-        inn = remote(away, gr.at[src], g_send.at[step], g_recv.at[step], at_quad(to))
-        return out, inn
-
-    for step in range(1, heads):
-        bias_out(step)[0].start()
-    gr[me] = gs[xi, core]
-
-    for step in range(1, heads):
-        out_quad(step)[1].wait_recv()
-    for array, ref in enumerate((dq_ref, dk_ref, dv_ref, dg_ref)):
-        for local in range(own_rows):
-            tall = jnp.concatenate([orecv[head, array, local] for head in range(heads)], axis=0)
-            ref[local] = jnp.transpose(tall.astype(jnp.float32)).astype(jnp.bfloat16)
-    for step in range(1, heads):
-        bias_out(step)[1].wait_recv()
-    db_ref[...] = gr[...].astype(jnp.float32)
-
-    for step in range(1, heads):
-        bias_quad(step)[0].wait_send()
-        out_quad(step)[0].wait_send()
-        bias_out(step)[0].wait_send()
-        for array in range(5):
-            in_quad(array, step)[0].wait_send()
+    for step in range(1, heads):
+        sum_out(step).start()
+    own_sum = pltpu.make_async_copy(gs.at[xi, core], gr.at[me], local_sem.at[2])
+    own_sum.start()
+
+    for step in range(1, heads):
+        grads_in(step).wait_recv()
+        sum_in(step).wait_recv()
+    own_grads.wait()
+    own_sum.wait()
+    for step in range(1, heads):
+        bias_out_of(step).wait_send()
+        grads_out(step).wait_send()
+        sum_out(step).wait_send()
+        for array in range(4):
+            token_out(array, step).wait_send()
     for step in range(1, groups):
-        index = lax.rem(zi + step, groups)
-        partial_out(index).wait_send()
+        for part in range(pair):
+            partial_out(lax.rem(zi + step, groups), part).wait_send()
     for index in range(groups):
-
-        @pl.when(jnp.logical_and(zi > 0, index >= zi))
-        def _(index=index):
-            to_left(index).wait_send()
-
-        @pl.when(jnp.logical_and(zi < groups - 1, index <= zi))
-        def _(index=index):
-            to_right(index).wait_send()
+        for part in range(pair):
+
+            @pl.when(jnp.logical_and(zi > 0, index >= zi))
+            def _(at=index * pair + part):
+                to_left(at).wait_send()
+
+            @pl.when(jnp.logical_and(zi < groups - 1, index <= zi))
+            def _(at=index * pair + part):
+                to_right(at).wait_send()
+
+
+def write_kernel(grads, sums, g_ref, o_ref, dq_ref, dk_ref, dv_ref, dg_ref, db_ref):
+    heads = grads.shape[0]
+    for local in range(g_ref.shape[0]):
+        for array, ref in enumerate((dq_ref, dk_ref, dv_ref, dg_ref)):
+            tall = jnp.concatenate([grads[head, array, local] for head in range(heads)], axis=0)
+            value = jnp.transpose(tall)
+            if array == 3:
+                sig = jax.nn.sigmoid(g_ref[local].astype(jnp.float32))
+                scale = o_ref[local].astype(jnp.float32) * sig * (1.0 - sig)
+                value = (value.astype(jnp.float32) * scale).astype(jnp.bfloat16)
+            ref[local] = value
+    db_ref[...] = sums[...].astype(jnp.float32)
 
 
 def fused(row_size, cores, query, keys, values, gate_logits, pair_bias, key_mask, grad_out):
@@ -398,20 +455,23 @@
     blocks = groups * pair
     low, full, dma = jnp.bfloat16, jnp.float32, pltpu.SemaphoreType.DMA
     grad = jax.ShapeDtypeStruct(query.shape, low)
-    vmem = pl.BlockSpec(memory_space=pltpu.VMEM)
-    return pl.pallas_call(
+    vmem, place = pl.BlockSpec(memory_space=pltpu.VMEM), pl.BlockSpec(memory_space=pl.ANY)
+    grads, sums = pl.pallas_call(
         functools.partial(fused_kernel, groups, pair, cores),
-        out_shape=(grad, grad, grad, grad, jax.ShapeDtypeStruct(pair_bias.shape, full)),
-        in_specs=[vmem] * 7,
-        out_specs=[vmem] * 5,
+        out_shape=(
+            jax.ShapeDtypeStruct((heads, 4, own_rows, width, tokens), low),
+            jax.ShapeDtypeStruct((heads, block, tokens), low),
+        ),
+        in_specs=[vmem] * 5 + [place, vmem],
+        out_specs=[place] * 2,
         scratch_shapes=[
-            pltpu.VMEM((5, heads, own_rows, width, tokens), low),
-            pltpu.VMEM((5, pair, cores, own_rows, width, tokens), low),
+            pltpu.VMEM((4, heads, own_rows, width, tokens), low),
+            pltpu.VMEM((4, pair, cores, own_rows, width, tokens), low),
+            pltpu.VMEM((1, tokens), jnp.int32),
             pltpu.VMEM((cores, 1, tokens), jnp.int32),
             pltpu.VMEM((blocks, cores, block, tokens), low),
             pltpu.VMEM((rows, whole, width), low),
             pltpu.VMEM((rows, whole, width), low),
-            pltpu.VMEM((rows, whole, width), full),
             pltpu.VMEM((rows, whole, width), full),
             pltpu.VMEM((rows, whole, width), full),
             pltpu.VMEM((rows, width, whole), full),
@@ -419,18 +479,23 @@
             pltpu.VMEM((blocks, cores, block, tokens), low),
             pltpu.VMEM((groups, pair, cores, block, tokens), low),
             pltpu.VMEM((pair, cores, block, tokens), low),
-            pltpu.VMEM((heads, block, tokens), low),
             pltpu.VMEM((pair, cores, 4, own_rows, width, tokens), low),
-            pltpu.VMEM((heads, 4, own_rows, width, tokens), low),
-            dma((5, heads)), dma((5, heads)), dma((heads,)), dma((heads,)),
+            dma((4, heads)), dma((4, heads)), dma((heads,)), dma((heads,)),
             dma((cores,)), dma((cores,)),
-            dma((groups,)), dma((groups,)), dma((groups,)), dma((groups,)), dma((groups,)),
-            dma((heads,)), dma((heads,)), dma((heads,)), dma((heads,)),
+            dma((blocks,)), dma((blocks,)), dma((blocks,)),
+            dma((groups, pair)), dma((groups, pair)),
+            dma((heads,)), dma((heads,)), dma((heads,)), dma((heads,)), dma((3,)),
         ],
         compiler_params=pltpu.CompilerParams(
             collective_id=0, has_side_effects=True, vmem_limit_bytes=58 << 20
         ),
-    )(query, keys, values, gate_logits, grad_out, pair_bias, key_mask.reshape(1, tokens))
+    )(query, keys, values, gate_logits, grad_out, pair_bias, key_mask)
+    return pl.pallas_call(
+        write_kernel,
+        out_shape=(grad, grad, grad, grad, jax.ShapeDtypeStruct(pair_bias.shape, full)),
+        in_specs=[vmem] * 4,
+        out_specs=[vmem] * 5,
+    )(grads, sums, gate_logits, grad_out)
 
 
 def solution(mesh):

time: 79.2 us -> 64.2 us (0.81)
  Pallas kernels: 72.2 us -> 63.4 us
  local copies, waits for them, and re-layouts: 6.09 us -> 0 us
    pallas_call x1, Pallas kernels: 72.2 us -> 60.8 us  [fused(): pl.pallas_call(functools.partial(fused_kernel, groups, pair, cores), out_...]
    unnamed x13 -> x0, local copies, waits for them, and re-layouts: 4.84 us -> none
    pallas_call x0 -> x1, Pallas kernels: none -> 2.58 us  [fused(): pl.pallas_call(write_kernel, out_shape=(grad, grad, grad, grad, jax.Shape...]
    reshape x1 -> x0, local copies, waits for them, and re-layouts: 1.25 us -> none  [fused(): key_mask.reshape(1, tokens)]
where the time goes in v2:
time: 64.2 us; the launch traced here: 64 us
  Pallas kernels  63.4 us (99%)
    pallas_call x1, Pallas kernels, fused(): pl.pallas_call(functools.partial(fused_kernel, groups, pair, cores), out_...  60.8 us
    pallas_call x1, Pallas kernels, fused(): pl.pallas_call(write_kernel, out_shape=(grad, grad, grad, grad, jax.Shape...  2.58 us

profile of v2, /device:TPU:29, one launch (start us, length us, event | category | flops | bytes accessed | tf_op | source)
XLA Modules:
  0.0 64.0 jit_solution(15553967274923552995)
XLA Ops:
  0.6 60.8 %shard_map.110 = (bf16[4,4,2,32,384]{4,3,2,1,0:T(8,128)(2,1)}, bf16[4,96,384]{2,1,0:T(8,128)(2,1)}) custom-call(bf16[2,384,128]{2,1,0:T(8,128)(2,1)} %q_ref.1, bf16[2,384,128]{2,1,0:T(8,128)(2,1)} %k_ref.1, bf16[2,384,128]{2,1,0:T(8,128)(2,1)} %v_ref.1, bf16[2,384,128]{2,1,0:T(8,128)(2,1)} %g_ref.3, bf16[2,384,128]{2,1,0:T(8,128)(2,1)} %o_ref.3, ...), custom_call_target="tpu_custom_call" | custom-call | tf_op jit(solution)/shard_map/pallas_call | solution.py:459
  61.5 2.6 %shard_map.111 = (bf16[2,384,128]{2,1,0:T(8,128)(2,1)}, bf16[2,384,128]{2,1,0:T(8,128)(2,1)}, bf16[2,384,128]{2,1,0:T(8,128)(2,1)}, bf16[2,384,128]{2,1,0:T(8,128)(2,1)}, f32[4,96,384]{2,1,0:T(8,128)}) custom-call(bf16[4,4,2,32,384]{4,3,2,1,0:T(8,128)(2,1)} %get-tuple-element.7.grads, bf16[4,96,384]{2,1,0:T(8,128)(2,1)} %get-tuple-element.8.sums, ...), custom_call_target="tpu_custom_call" | custom-call | tf_op jit(solution)/shard_map/pallas_call | solution.py:493

commit v3 on v2

--- a/solution.py
+++ b/solution.py
@@ -284,11 +284,15 @@
         dk_acc[index] = jnp.zeros((width, keys), jnp.float32)
         dv_acc[index] = jnp.zeros((width, keys), jnp.float32)
 
-    def queries(rblk):
+    def queries(blk):
         mask = jnp.concatenate([mb[c] for c in range(cores)], axis=1).astype(jnp.float32)
-        bias = jnp.concatenate([bb[rblk, c] for c in range(cores)], axis=1).astype(jnp.float32)
+        parts = [
+            jnp.concatenate([bb[blk * pair + part, c] for c in range(cores)], axis=1)
+            for part in range(pair)
+        ]
+        bias = jnp.concatenate(parts, axis=0).astype(jnp.float32)
         bias = bias + 1000000000.0 * (mask - 1.0)
-        here = pl.ds(pl.multiple_of(rblk * block, 32), block)
+        here = pl.ds(pl.multiple_of(blk * pair * block, 32), pair * block)
         total = None
         for index in range(rows):
             kt, vt = joined(1, index), joined(2, index)
@@ -306,8 +310,10 @@
             dk_acc[index] += tn(q, d_low)
             dv_acc[index] += tn(da, low)
             total = d_logits if total is None else total + d_logits
-        for c in range(cores):
-            sb[rblk, c] = total[:, c * tokens : (c + 1) * tokens].astype(jnp.bfloat16)
+        for part in range(pair):
+            rows_of = total[part * block : (part + 1) * block].astype(jnp.bfloat16)
+            for c in range(cores):
+                sb[blk * pair + part, c] = rows_of[:, c * tokens : (c + 1) * tokens]
 
     def partial_out(index, part):
         return remote(
@@ -332,8 +338,8 @@
             for s in range(groups):
                 hit = jnp.logical_and(zi == a, step == s)
                 index = jnp.where(hit, orders[a][s], index)
+        queries(index)
         for part in range(pair):
-            queries(index * pair + part)
 
             @pl.when(index != zi)
             def _(part=part):

time: 64.2 us -> 62.6 us (0.975)
  Pallas kernels: 63.4 us -> 61.8 us
    pallas_call x1, Pallas kernels: 60.8 us -> 59.2 us  [fused(): pl.pallas_call(functools.partial(fused_kernel, groups, pair, cores), out_...]
where the time goes in v3:
time: 62.6 us; the launch traced here: 62.4 us
  Pallas kernels  61.8 us (99%)
  between operations  0.64 us (1%)
    pallas_call x1, Pallas kernels, fused(): pl.pallas_call(functools.partial(fused_kernel, groups, pair, cores), out_...  59.2 us
    pallas_call x1, Pallas kernels, fused(): pl.pallas_call(write_kernel, out_shape=(grad, grad, grad, grad, jax.Shape...  2.58 us

profile of v3, /device:TPU:29, one launch (start us, length us, event | category | flops | bytes accessed | tf_op | source)
XLA Modules:
  0.0 62.4 jit_solution(2273965477393060740)
XLA Ops:
  0.6 59.2 %shard_map.110 = (bf16[4,4,2,32,384]{4,3,2,1,0:T(8,128)(2,1)}, bf16[4,96,384]{2,1,0:T(8,128)(2,1)}) custom-call(bf16[2,384,128]{2,1,0:T(8,128)(2,1)} %q_ref.1, bf16[2,384,128]{2,1,0:T(8,128)(2,1)} %k_ref.1, bf16[2,384,128]{2,1,0:T(8,128)(2,1)} %v_ref.1, bf16[2,384,128]{2,1,0:T(8,128)(2,1)} %g_ref.3, bf16[2,384,128]{2,1,0:T(8,128)(2,1)} %o_ref.3, ...), custom_call_target="tpu_custom_call" | custom-call | tf_op jit(solution)/shard_map/pallas_call | solution.py:465
  59.9 2.6 %shard_map.111 = (bf16[2,384,128]{2,1,0:T(8,128)(2,1)}, bf16[2,384,128]{2,1,0:T(8,128)(2,1)}, bf16[2,384,128]{2,1,0:T(8,128)(2,1)}, bf16[2,384,128]{2,1,0:T(8,128)(2,1)}, f32[4,96,384]{2,1,0:T(8,128)}) custom-call(bf16[4,4,2,32,384]{4,3,2,1,0:T(8,128)(2,1)} %get-tuple-element.7.grads, bf16[4,96,384]{2,1,0:T(8,128)(2,1)} %get-tuple-element.8.sums, ...), custom_call_target="tpu_custom_call" | custom-call | tf_op jit(solution)/shard_map/pallas_call | solution.py:499

commit v4 on v3

--- a/solution.py
+++ b/solution.py
@@ -343,7 +343,7 @@
 
             @pl.when(index != zi)
             def _(part=part):
-                partial_out(index, part).start()
+                partial_out(index, lax.rem(xi + 1 + part, pair)).start()
 
         return carry
 
@@ -395,7 +395,8 @@
     own_grads = pltpu.make_async_copy(ot.at[xi, core], orecv.at[me], local_sem.at[1])
     own_grads.start()
 
-    for part in range(pair):
+    for turn_of in range(pair):
+        part = lax.rem(xi + 1 + turn_of, pair)
         for step in range(1, groups):
             src = lax.rem(zi + step, groups)
             remote(
@@ -407,8 +408,13 @@
             for step in range(1, groups):
                 value += rb[lax.rem(zi + step, groups), part, c].astype(jnp.float32)
             gs[part, c] = value.astype(jnp.bfloat16)
-    for step in range(1, heads):
-        sum_out(step).start()
+        if turn_of < pair - 1:
+            for c in range(cores):
+                sum_out(lax.rem(part * cores + c + heads - me, heads)).start()
+        else:
+            for c in range(1, cores):
+                to = part * cores + lax.rem(core + c, cores)
+                sum_out(lax.rem(to + heads - me, heads)).start()
     own_sum = pltpu.make_async_copy(gs.at[xi, core], gr.at[me], local_sem.at[2])
     own_sum.start()
 

time: 62.6 us -> 59.7 us (0.954)
  Pallas kernels: 61.8 us -> 58.6 us
    pallas_call x1, Pallas kernels: 59.2 us -> 56.1 us  [fused(): pl.pallas_call(functools.partial(fused_kernel, groups, pair, cores), out_...]
where the time goes in v4:
time: 59.7 us; the launch traced here: 59.3 us
  Pallas kernels  58.6 us (98%)
  between operations  0.64 us (1%)
    pallas_call x1, Pallas kernels, fused(): pl.pallas_call(functools.partial(fused_kernel, groups, pair, cores), out_...  56.1 us
    pallas_call x1, Pallas kernels, fused(): pl.pallas_call(write_kernel, out_shape=(grad, grad, grad, grad, jax.Shape...  2.58 us

profile of v4, /device:TPU:29, one launch (start us, length us, event | category | flops | bytes accessed | tf_op | source)
XLA Modules:
  0.0 59.3 jit_solution(15728949166793279315)
XLA Ops:
  0.6 56.1 %shard_map.110 = (bf16[4,4,2,32,384]{4,3,2,1,0:T(8,128)(2,1)}, bf16[4,96,384]{2,1,0:T(8,128)(2,1)}) custom-call(bf16[2,384,128]{2,1,0:T(8,128)(2,1)} %q_ref.1, bf16[2,384,128]{2,1,0:T(8,128)(2,1)} %k_ref.1, bf16[2,384,128]{2,1,0:T(8,128)(2,1)} %v_ref.1, bf16[2,384,128]{2,1,0:T(8,128)(2,1)} %g_ref.3, bf16[2,384,128]{2,1,0:T(8,128)(2,1)} %o_ref.3, ...), custom_call_target="tpu_custom_call" | custom-call | tf_op jit(solution)/shard_map/pallas_call | solution.py:471
  56.7 2.6 %shard_map.111 = (bf16[2,384,128]{2,1,0:T(8,128)(2,1)}, bf16[2,384,128]{2,1,0:T(8,128)(2,1)}, bf16[2,384,128]{2,1,0:T(8,128)(2,1)}, bf16[2,384,128]{2,1,0:T(8,128)(2,1)}, f32[4,96,384]{2,1,0:T(8,128)}) custom-call(bf16[4,4,2,32,384]{4,3,2,1,0:T(8,128)(2,1)} %get-tuple-element.7.grads, bf16[4,96,384]{2,1,0:T(8,128)(2,1)} %get-tuple-element.8.sums, ...), custom_call_target="tpu_custom_call" | custom-call | tf_op jit(solution)/shard_map/pallas_call | solution.py:505
